TPU v7x, 32 devices: a whole 2x2x4 slice. The times are simulated.
32 devices in a mesh: row: 8 (over y, x, core), col: 4 (over z).
Axes of the slice: x: 2, y: 2, z: 4, core: 2. Of those that a mesh axis runs over, the one named last changes fastest.
Arguments:
- pair: bfloat16 [256, 256, 128], P('row', 'col'), may hold values from -6 to 6
- cotangent: bfloat16 [256, 256, 128], P('row', 'col'), may hold values from -6 to 6
- length: int32 [1], replicated, may hold values from 128 to 256
- norm_gain: float32 [128], replicated, may hold values from 0.1 to 1.9
- norm_bias: float32 [128], replicated, may hold values from -1.5 to 1.5
- left_weight: bfloat16 [128, 256], replicated, may hold values from -0.5 to 0.5
- right_weight: bfloat16 [128, 256], replicated, may hold values from -0.5 to 0.5
- gate_weight: bfloat16 [128, 128], replicated, may hold values from -0.5 to 0.5
- out_gain: float32 [128], replicated, may hold values from 0.1 to 1.9
- out_bias: float32 [128], replicated, may hold values from -2 to 2
- out_weight: bfloat16 [128, 128], replicated, may hold values from -0.5 to 0.5
Outputs:
- update: bfloat16 [256, 256, 128], P('row', 'col')
- grad_pair: bfloat16 [256, 256, 128], P('row', 'col')
- grad_left: float32 [128, 256], replicated
- grad_right: float32 [128, 256], replicated
- grad_gating: float32 [128, 128], replicated
- grad_output: float32 [128, 128], replicated
- grad_norms: float32 [4, 128], replicated
Inputs may be any that keep to these rules, and one draw needn't show every extreme that they name: Tokens at positions 255 down to length are padding.
All inputs are finite; a program needn't handle non-finite values.
Results may differ from a plain program's by a relative error of at most 0.014.
Values may be sent and summed in bfloat16 or wider, within the bound.
No kernel may reach another device: no remote copies, remote signals or barrier semaphores. Data moves between devices by JAX's collectives and lax.ppermute only.
A program may use at most 128 MiB of HBM per device.

v0:
```python
import jax
import jax.numpy as jnp
from jax import lax
from jax.sharding import PartitionSpec as P

EPS = 1e-05


def broadcast(block, axis, holder):
    block = jnp.where(lax.axis_index(axis) == holder, block, jnp.zeros_like(block))
    return lax.psum(block, axis)


def normalize(values):
    center = values - jnp.mean(values, axis=-1, keepdims=True)
    inverse = lax.rsqrt(jnp.mean(center * center, axis=-1, keepdims=True) + EPS)
    return (center * inverse, inverse)


def gating(panel, weight, first_ok, second_ok, hidden):
    projected = jnp.einsum("ikc,ch->ikh", panel, weight, preferred_element_type=jnp.float32)
    values = projected[..., :hidden]
    sigmoid_val = jax.nn.sigmoid(projected[..., hidden:])
    pad_mask = (first_ok[:, None] & second_ok[None, :]).astype(jnp.float32)[..., None]
    return ((pad_mask * sigmoid_val * values).astype(jnp.bfloat16), values, sigmoid_val, pad_mask)


def push_back(partial_value, values, sigmoid_val, pad_mask, weight, panel):
    combined = jnp.concatenate(
        [
            partial_value * pad_mask * sigmoid_val,
            partial_value * pad_mask * values * sigmoid_val * (1.0 - sigmoid_val),
        ],
        axis=-1,
    ).astype(jnp.bfloat16)
    panel_grad = jnp.einsum("ikh,ch->ikc", combined, weight, preferred_element_type=jnp.float32)
    weight_grad = jnp.einsum("ikc,ikh->ch", panel, combined, preferred_element_type=jnp.float32)
    return (panel_grad, weight_grad)


def per_device(
    pair,
    cotangent,
    length,
    norm_gain,
    norm_bias,
    left_weight,
    right_weight,
    gate_weight,
    out_gain,
    out_bias,
    out_weight,
):
    row_index = lax.axis_index("row")
    col_index = lax.axis_index("col")
    n_row = lax.axis_size("row")
    n_col = lax.axis_size("col")
    per_col = n_row // n_col
    rows_dev = pair.shape[0]
    cols_dev = pair.shape[1]
    tokens = rows_dev * n_row
    hidden = out_weight.shape[0]
    pair_hat, pair_scale = normalize(pair.astype(jnp.float32))
    normed = (pair_hat * norm_gain + norm_bias).astype(jnp.bfloat16)
    real_count = length[0]
    second_ok = jnp.arange(tokens, dtype=jnp.int32) < real_count
    own_ok = row_index * rows_dev + jnp.arange(rows_dev, dtype=jnp.int32) < real_count
    partner_ok = col_index * cols_dev + jnp.arange(cols_dev, dtype=jnp.int32) < real_count
    left_tile, left_val, left_sig, tile_mask = gating(
        normed, left_weight, own_ok, partner_ok, hidden
    )
    right_tile, right_val, right_sig, unused_mask = gating(
        normed, right_weight, own_ok, partner_ok, hidden
    )
    row_panel = lax.all_gather(normed, "col", axis=1, tiled=True)
    pieces = []
    for member in range(per_col):
        pieces.append(broadcast(row_panel, "row", col_index * per_col + member))
    col_panel = jnp.concatenate(pieces, axis=0)
    left_act = gating(row_panel, left_weight, own_ok, second_ok, hidden)[0]
    right_act = gating(col_panel, right_weight, partner_ok, second_ok, hidden)[0]
    tri = jnp.einsum("ikh,jkh->ijh", left_act, right_act, preferred_element_type=jnp.float32)
    tri_hat, tri_scale = normalize(tri)
    tri_normed = (tri_hat * out_gain + out_bias).astype(jnp.bfloat16)
    outer_val = jnp.einsum(
        "ijh,hc->ijc", tri_normed, out_weight, preferred_element_type=jnp.float32
    )
    gate_val = jax.nn.sigmoid(
        jnp.einsum("ijc,cd->ijd", normed, gate_weight, preferred_element_type=jnp.float32)
    )
    update = (gate_val * outer_val).astype(jnp.bfloat16)
    upstream = cotangent.astype(jnp.float32)
    outer_grad = (upstream * gate_val).astype(jnp.bfloat16)
    gate_grad = (upstream * outer_val * gate_val * (1.0 - gate_val)).astype(jnp.bfloat16)
    grad_output = jnp.einsum(
        "ijh,ijc->hc", tri_normed, outer_grad, preferred_element_type=jnp.float32
    )
    grad_gating = jnp.einsum("ijc,ijd->cd", normed, gate_grad, preferred_element_type=jnp.float32)
    tnorm_grad = jnp.einsum(
        "ijc,hc->ijh", outer_grad, out_weight, preferred_element_type=jnp.float32
    )
    hat_grad = tnorm_grad * out_gain
    tri_grad = (
        tri_scale
        * (
            hat_grad
            - jnp.mean(hat_grad, axis=-1, keepdims=True)
            - tri_hat * jnp.mean(hat_grad * tri_hat, axis=-1, keepdims=True)
        )
    ).astype(jnp.bfloat16)
    row_partial = jnp.einsum(
        "ijh,jkh->ikh", tri_grad, right_act, preferred_element_type=jnp.float32
    )
    col_partial = jnp.einsum("ijh,ikh->jkh", tri_grad, left_act, preferred_element_type=jnp.float32)
    row_part = lax.psum_scatter(
        row_partial.astype(jnp.bfloat16), "col", scatter_dimension=1, tiled=True
    ).astype(jnp.float32)
    summed = lax.psum_scatter(
        col_partial.astype(jnp.bfloat16), "row", scatter_dimension=0, tiled=True
    )
    slab = summed[None]
    received = lax.all_to_all(slab, "col", split_axis=2, concat_axis=0, tiled=True)
    select = (jnp.arange(per_col, dtype=jnp.int32) == row_index // n_col).astype(jnp.bfloat16)
    spread = (received[:, None] * select[None, :, None, None, None]).reshape(
        (n_row,) + received.shape[1:]
    )
    returned = lax.all_to_all(spread, "row", split_axis=0, concat_axis=0, tiled=True)
    start = row_index % per_col * n_col
    owned = lax.dynamic_slice_in_dim(returned, start, n_col, 0).reshape(rows_dev, cols_dev, -1)
    col_part = owned.astype(jnp.float32)
    from_rows, grad_left = push_back(row_part, left_val, left_sig, tile_mask, left_weight, normed)
    from_cols, grad_right = push_back(
        col_part, right_val, right_sig, tile_mask, right_weight, normed
    )
    gate_back = jnp.einsum(
        "ijd,cd->ijc", gate_grad, gate_weight, preferred_element_type=jnp.float32
    )
    normed_grad = gate_back + from_rows + from_cols
    scaled = normed_grad * norm_gain
    grad_pair = (
        pair_scale
        * (
            scaled
            - jnp.mean(scaled, axis=-1, keepdims=True)
            - pair_hat * jnp.mean(scaled * pair_hat, axis=-1, keepdims=True)
        )
    ).astype(jnp.bfloat16)
    grad_norms = jnp.stack(
        [
            jnp.sum(normed_grad * pair_hat, axis=(0, 1)),
            jnp.sum(normed_grad, axis=(0, 1)),
            jnp.sum(tnorm_grad * tri_hat, axis=(0, 1)),
            jnp.sum(tnorm_grad, axis=(0, 1)),
        ]
    )
    totals = lax.psum((grad_left, grad_right, grad_gating, grad_output, grad_norms), ("row", "col"))
    inverse = 1.0 / tokens
    return (
        update,
        grad_pair,
        totals[0] * inverse,
        totals[1] * inverse,
        totals[2] * inverse,
        totals[3] * inverse,
        totals[4] * inverse,
    )


def solution(mesh):
    return jax.shard_map(
        per_device,
        mesh=mesh,
        in_specs=(
            P("row", "col", None),
            P("row", "col", None),
            P(),
            P(),
            P(),
            P(),
            P(),
            P(),
            P(),
            P(),
            P(),
        ),
        out_specs=(P("row", "col", None), P("row", "col", None), P(), P(), P(), P(), P()),
        check_vma=False,
    )
```

profile of v0, /device:TPU:0, one launch (start us, length us, event | category | flops | bytes accessed | tf_op | source)
XLA Modules:
  0.0 473.8 jit_solution(4896643660126480447)
XLA Ops:
  7.2 1.4 convert_reduce_fusion
  8.6 1.7 fusion.31
  10.3 2.5 fusion.25
  12.9 1.5 fusion.17
  14.4 47.0 %all-gather.2.cloned.1.call-done = bf16[32,256,128]{2,1,0:T(8,128)(2,1)} async-done(((bf16[32,64,128]{2,1,0:T(8,128)(2,1)}), bf16[32,256,128]{2,1,0:T(8,128)(2,1)}) %all-gather.2.cloned.1.call-update) | async-done | bytes 2097168 | tf_op jit(solution)/shard_map/all_gather | solution.py:75
  61.4 3.8 broadcast_select_fusion.1
  66.2 1.3 fusion.73
  68.3 3.1 copy.54
  71.5 2.8 fusion.53
  74.4 2.7 fusion.5
  77.0 4.6 copy.52
  81.6 63.4 %all-reduce.7.cloned.1.call-done = (bf16[32,256,128]{2,1,0:T(8,128)(2,1)}, bf16[32,256,128]{2,1,0:T(8,128)(2,1)}) async-done(((bf16[32,256,128]{2,1,0:T(8,128)(2,1)}, bf16[32,256,128]{2,1,0:T(8,128)(2,1)}), (bf16[32,256,128]{2,1,0:T(8,128)(2,1)}, bf16[32,256,128]{2,1,0:T(8,128)(2,1)})) %all-reduce.7.cloned.1.call-update) | async-done | bytes 4194320 | tf_op jit(solution)/shard_map/psum | solution.py:11
  145.1 4.5 fusion.10
  149.6 4.3 fusion
  154.0 6.8 %copy.51 = bf16[64,256,128]{1,0,2:T(8,128)(2,1)} copy(bf16[64,256,128]{2,1,0:T(8,128)(2,1)} %fusion) | data formatting | bytes 8388608 | tf_op jit(solution)/shard_map/convert_element_type | solution.py:25
  160.7 4.1 bitcast_reduce_fusion
  165.5 1.3 multiply_reduce_fusion
  166.8 1.8 multiply_convert_fusion
  168.6 1.3 fusion.74
  169.9 2.2 copy.66
  173.4 4.3 fusion.75
  177.7 4.6 copy.56
  182.5 41.1 %reduce-scatter.7.cloned.1.call-done = bf16[8,32768]{1,0:T(8,128)(2,1)} async-done(((bf16[64,32768]{1,0:T(8,128)(2,1)}), bf16[8,32768]{1,0:T(8,128)(2,1)}) %reduce-scatter.7.cloned.1.call-update) | async-done | bytes 524304
  223.6 1.2 copy.71
  225.1 1.3 copy.58
  226.4 4.6 all-to-all-start
  231.1 1.8 fusion.51
  232.9 1.7 fusion.56
  234.6 1.1 copy.53
  235.7 23.9 %all-to-all-done = bf16[1,8,256,128]{3,1,0,2:T(8,128)(2,1)} async-done(((bf16[1,8,256,128]{3,1,0,2:T(8,128)(2,1)}), bf16[1,8,256,128]{3,1,0,2:T(8,128)(2,1)}, u32[]{:S(2)}, u32[]{:S(2)}) %all-to-all-start) | async-done | bytes 524320 | tf_op jit(solution)/shard_map/all_to_all | solution.py:122
  259.6 1.2 copy.60
  260.8 1.1 bitcast_multiply_fusion
  261.9 4.2 all-to-all-start.1
  266.2 1.2 fusion.34
  269.7 11.9 %all-to-all-done.1 = bf16[8,8,64,128]{3,2,1,0:T(8,128)(2,1)} async-done(((bf16[8,8,64,128]{3,2,1,0:T(8,128)(2,1)}), bf16[8,8,64,128]{3,2,1,0:T(8,128)(2,1)}, u32[]{:S(2)}, u32[]{:S(2)}) %all-to-all-start.1) | async-done | bytes 1048608 | tf_op jit(solution)/shard_map/all_to_all | solution.py:127
  281.5 1.1 constant_dynamic-slice_fusion
  282.7 2.8 fusion.49
  285.5 1.0 convolution_bitcast_fusion.1
  286.5 1.4 convolution_add_fusion.1
  287.9 1.0 convolution_bitcast_fusion
  289.0 2.6 fusion.30
  291.6 37.2 %psum.55 = f32[4,128]{1,0:T(4,128)S(1)} all-reduce(f32[4,128]{1,0:T(4,128)S(1)} %pad_maximum_fusion.6), channel_id=1, replica_groups=mesh['row'=8,'col'=4] {'row','col'}, use_global_device_ids=true, to_apply=%region_20.21 | all-reduce | flops 512 | bytes 4096 | tf_op jit(solution)/shard_map/psum | solution.py:156
  328.8 1.9 fusion.29
  331.3 129.8 %all-reduce.5.cloned.1.call-done = (f32[128,256]{1,0:T(8,128)}, f32[128,256]{1,0:T(8,128)}, f32[128,128]{1,0:T(8,128)}, f32[128,128]{1,0:T(8,128)}) async-done(((f32[128,256]{1,0:T(8,128)}, f32[128,256]{1,0:T(8,128)}, f32[128,128]{1,0:T(8,128)}, f32[128,128]{1,0:T(8,128)}), (f32[128,256]{1,0:T(8,128)}, f32[128,256]{1,0:T(8,128)}, f32[128,128]{1,0:T(8,128)}, ...) | async-done | bytes 393232 | tf_op jit(solution)/shard_map/psum | solution.py:156
  461.2 1.6 broadcast_multiply_fusion
  462.7 1.6 broadcast_multiply_fusion.1
  464.3 1.5 broadcast_multiply_fusion.2
  465.8 1.5 broadcast_multiply_fusion.3
  (66 shorter events, 6.6 us)
Async XLA Ops:
  7.2 137.9 %copy-start = (bf16[128,256]{1,0:T(8,128)(2,1)S(1)}, bf16[128,256]{1,0:T(8,128)(2,1)}, u32[]{:S(2)}) copy-start(bf16[128,256]{1,0:T(8,128)(2,1)} %param.17) | copy-start | bytes 196612
  7.2 5.7 %copy-start.12 = (bf16[128,128]{1,0:T(8,128)(2,1)S(1)}, bf16[128,128]{1,0:T(8,128)(2,1)}, u32[]{:S(2)}) copy-start(bf16[128,128]{1,0:T(8,128)(2,1)} %param.18) | copy-start | bytes 98308
  7.2 54.2 %all-gather.2.cloned.1.call-start = ((), (), s32[]{:S(2)}) async-start(), calls=%async_computation.4 | async-start | bytes 2621440 | tf_op jit(solution)/shard_map/all_gather | solution.py:75
  12.8 132.2 %all-reduce.7.cloned.1.call-start = ((), (), s32[]{:S(2)}) async-start(), calls=%async_computation.8 | async-start | bytes 8388608 | tf_op jit(solution)/shard_map/psum | solution.py:11
  65.2 1.0 copy-start.6
  65.2 1.0 copy-start.11
  65.2 158.4 %reduce-scatter.7.cloned.1.call-start = ((), (), s32[]{:S(2)}) async-start(), calls=%async_computation.6 | async-start | bytes 4718592
  67.6 4.0 copy-start.9
  164.8 0.7 copy-start.14
  165.5 1.3 copy-start.15
  166.8 1.8 copy-start.1
  168.6 1.3 copy-start.3
  172.2 1.2 copy-start.4
  172.2 110.4 %reduce-scatter.5.cloned.1.call-start = ((), (), s32[]{:S(2)}) async-start(), calls=%async_computation.5 | async-start | bytes 2621440 | tf_op jit(solution)/shard_map/reduce_scatter | solution.py:115
  223.6 7.5 %copy-start.2 = (bf16[32,64,128]{2,1,0:T(8,128)(2,1)S(1)}, bf16[32,64,128]{2,1,0:T(8,128)(2,1)}, u32[]{:S(2)}) copy-start(bf16[32,64,128]{2,1,0:T(8,128)(2,1)} %fusion.25) | copy-start | bytes 1572868
  226.4 33.2 %all-to-all-start = ((bf16[1,8,256,128]{3,1,0,2:T(8,128)(2,1)}), bf16[1,8,256,128]{3,1,0,2:T(8,128)(2,1)}, u32[]{:S(2)}, u32[]{:S(2)}) async-start(bf16[1,8,256,128]{3,1,0,2:T(8,128)(2,1)} %copy.58), calls=%async_computation.1 | async-start | bytes 1048576 | tf_op jit(solution)/shard_map/all_to_all | solution.py:122
  231.1 3.5 copy-start.8
  260.8 5.4 %copy-start.7 = (bf16[32,64,128]{2,1,0:T(8,128)(2,1)S(1)}, bf16[32,64,128]{2,1,0:T(8,128)(2,1)}, u32[]{:S(2)}) copy-start(bf16[32,64,128]{2,1,0:T(8,128)(2,1)} %param.12) | copy-start | bytes 1572868
  261.9 19.6 %all-to-all-start.1 = ((bf16[8,8,64,128]{3,2,1,0:T(8,128)(2,1)}), bf16[8,8,64,128]{3,2,1,0:T(8,128)(2,1)}, u32[]{:S(2)}, u32[]{:S(2)}) async-start(bf16[8,8,64,128]{3,2,1,0:T(8,128)(2,1)} %bitcast_multiply_fusion), calls=%async_computation.2 | async-start | bytes 2097152 | tf_op jit(solution)/shard_map/all_to_all | solution.py:127
  266.2 195.0 %all-reduce.5.cloned.1.call-start = ((), (), s32[]{:S(2)}) async-start(), calls=%async_computation.7 | async-start | bytes 786432 | tf_op jit(solution)/shard_map/psum | solution.py:156
  285.5 2.5 copy-start.10
  286.5 2.5 copy-start.5
  286.5 2.5 copy-start.13
Sparse Core Ops, SparseCore 0:
  13.0 48.3 all-gather.1
  65.4 79.6 all-reduce.6
  172.3 51.2 reduce-scatter.6
  225.7 51.5 reduce-scatter.4
  330.9 130.2 all-reduce.4
where the time goes:
time: 475 us; the launch traced here: 474 us
  waiting for transfers between devices  317 us (67%)
  blocking collectives  37.2 us (8%)
  matrix products  32.8 us (7%)
  other arithmetic  32.6 us (7%)
  local copies, waits for them, and re-layouts  29.7 us (6%)
  between operations  14.8 us (3%)
  starting transfers between devices  9.43 us (2%)
    psum x1, waiting for transfers between devices, per_device(): lax.psum((grad_left, grad_right, grad_gating, grad_output, grad_norms), (...  130 us
    psum x1, waiting for transfers between devices, broadcast(): return lax.psum(block, axis)  63.4 us
    all_gather x1, waiting for transfers between devices, per_device(): row_panel = lax.all_gather(normed, 'col', axis=1, tiled=True)  47 us
    unnamed x6, waiting for transfers between devices  41.2 us
    psum x1, blocking collectives, per_device(): lax.psum((grad_left, grad_right, grad_gating, grad_output, grad_norms), (...  37.2 us
    all_to_all x1, waiting for transfers between devices, per_device(): lax.all_to_all(slab, 'col', split_axis=2, concat_axis=0, tiled=True)  23.9 us
    all_to_all x1, waiting for transfers between devices, per_device(): lax.all_to_all(spread, 'row', split_axis=0, concat_axis=0, tiled=True)  11.9 us
    convert_element_type x2, local copies, waits for them, and re-layouts, gating(): (pad_mask * sigmoid_val * values).astype(jnp.bfloat16)  11.4 us
  transfers between devices with their start and end apart: 7, of which 6 were waited for; matrix products, arithmetic and copies ran while one was open for 8% of the time, Pallas kernels for 0%

commit v1 on v0

--- a/solution.py
+++ b/solution.py
@@ -153,7 +153,9 @@
             jnp.sum(tnorm_grad, axis=(0, 1)),
         ]
     )
-    totals = lax.psum((grad_left, grad_right, grad_gating, grad_output, grad_norms), ("row", "col"))
+    totals = jax.lax.psum(
+        jax.lax.psum((grad_left, grad_right, grad_gating, grad_output, grad_norms), "row"), "col"
+    )
     inverse = 1.0 / tokens
     return (
         update,

time: 475 us -> 419 us (0.88)
  waiting for transfers between devices: 317 us -> 276 us
  blocking collectives: 37.2 us -> 22.1 us
    psum x1 -> x2, waiting for transfers between devices: 130 us -> 88.7 us  [the longest x1 52.4 us: per_device(): jax.lax.psum((grad_left, grad_right, grad_gating, grad_output, grad_norms...]
    psum x1 -> x2, blocking collectives: 37.2 us -> 22.1 us  [the longest x1 11.8 us: per_device(): jax.lax.psum((grad_left, grad_right, grad_gating, grad_output, grad_norms...]
    unnamed x6 -> x7, waiting for transfers between devices: 41.2 us -> 41.2 us
  transfers between devices with their start and end apart: 7 -> 8, of which waited for: 6 -> 7; matrix products, arithmetic and copies ran while one was open for 8% -> 10% of each run, Pallas kernels for 0% -> 0%
where the time goes in v1:
time: 419 us; the launch traced here: 418 us
  waiting for transfers between devices  276 us (66%)
  matrix products  32.8 us (8%)
  other arithmetic  32.6 us (8%)
  local copies, waits for them, and re-layouts  29.7 us (7%)
  blocking collectives  22.1 us (5%)
  between operations  15.1 us (4%)
  starting transfers between devices  9.47 us (2%)
    psum x1, waiting for transfers between devices, broadcast(): return lax.psum(block, axis)  63.4 us
    psum x1, waiting for transfers between devices, per_device(): jax.lax.psum((grad_left, grad_right, grad_gating, grad_output, grad_norms...  52.4 us
    all_gather x1, waiting for transfers between devices, per_device(): row_panel = lax.all_gather(normed, 'col', axis=1, tiled=True)  47 us
    unnamed x7, waiting for transfers between devices  41.2 us
    psum x1, waiting for transfers between devices, per_device(): jax.lax.psum(jax.lax.psum((grad_left, grad_right, grad_gating, grad_outpu...  36.3 us
    all_to_all x1, waiting for transfers between devices, per_device(): lax.all_to_all(slab, 'col', split_axis=2, concat_axis=0, tiled=True)  23.9 us
    all_to_all x1, waiting for transfers between devices, per_device(): lax.all_to_all(spread, 'row', split_axis=0, concat_axis=0, tiled=True)  11.9 us
    psum x1, blocking collectives, per_device(): jax.lax.psum((grad_left, grad_right, grad_gating, grad_output, grad_norms...  11.8 us
  transfers between devices with their start and end apart: 8, of which 7 were waited for; matrix products, arithmetic and copies ran while one was open for 10% of the time, Pallas kernels for 0%

profile of v1, /device:TPU:0, one launch (start us, length us, event | category | flops | bytes accessed | tf_op | source)
XLA Modules:
  0.0 417.9 jit_solution(13426788526660204223)
XLA Ops:
  7.2 1.4 convert_reduce_fusion
  8.6 1.7 fusion.31
  10.3 2.5 fusion.25
  12.9 1.5 fusion.17
  14.4 47.0 %all-gather.2.cloned.1.call-done = bf16[32,256,128]{2,1,0:T(8,128)(2,1)} async-done(((bf16[32,64,128]{2,1,0:T(8,128)(2,1)}), bf16[32,256,128]{2,1,0:T(8,128)(2,1)}) %all-gather.2.cloned.1.call-update) | async-done | bytes 2097168 | tf_op jit(solution)/shard_map/all_gather | solution.py:75
  61.4 3.8 broadcast_select_fusion.1
  66.2 1.3 fusion.73
  68.3 3.1 copy.54
  71.5 2.8 fusion.53
  74.4 2.7 fusion.5
  77.0 4.6 %copy.52 = bf16[32,256,128]{1,0,2:T(8,128)(2,1)} copy(bf16[32,256,128]{2,1,0:T(8,128)(2,1)} %fusion.5) | data formatting | bytes 4194304 | tf_op jit(solution)/shard_map/convert_element_type | solution.py:25
  81.6 63.4 %all-reduce.11.cloned.1.call-done = (bf16[32,256,128]{2,1,0:T(8,128)(2,1)}, bf16[32,256,128]{2,1,0:T(8,128)(2,1)}) async-done(((bf16[32,256,128]{2,1,0:T(8,128)(2,1)}, bf16[32,256,128]{2,1,0:T(8,128)(2,1)}), (bf16[32,256,128]{2,1,0:T(8,128)(2,1)}, bf16[32,256,128]{2,1,0:T(8,128)(2,1)})) %all-reduce.11.cloned.1.call-update) | async-done | bytes 4194320 | tf_op jit(solution)/shard_map/psum | solution.py:11
  145.1 4.5 %fusion.10 = f32[64,256,256]{2,1,0:T(8,128)S(1)} fusion(bf16[32,256,128]{2,1,0:T(8,128)(2,1)} %get-tuple-element.22, bf16[32,256,128]{2,1,0:T(8,128)(2,1)} %get-tuple-element.23, bf16[128,256]{1,0:T(8,128)(2,1)S(1)} %copy-done), kind=kOutput, calls=%fused_computation.14 | convolution fusion | flops 1075838976 | bytes 21037056 | tf_op jit(solution)/shard_map/ikc,ch->ikh/dot_general | solution.py:21
  149.6 4.3 %fusion = bf16[64,256,128]{2,1,0:T(8,128)(2,1)} fusion(f32[64,256,256]{2,1,0:T(8,128)S(1)} %fusion.10, f32[64,256]{1,0:T(8,128)S(1)} %and_convert_fusion), kind=kLoop, calls=%fused_computation.1 | loop fusion | flops 12582912 | bytes 21037056 | tf_op jit(solution)/shard_map/convert_element_type | solution.py:25
  154.0 6.8 %copy.51 = bf16[64,256,128]{1,0,2:T(8,128)(2,1)} copy(bf16[64,256,128]{2,1,0:T(8,128)(2,1)} %fusion) | data formatting | bytes 8388608 | tf_op jit(solution)/shard_map/convert_element_type | solution.py:25
  160.7 4.1 bitcast_reduce_fusion
  165.5 1.3 multiply_reduce_fusion
  166.8 1.8 multiply_convert_fusion
  168.6 1.3 fusion.74
  169.9 2.2 copy.66
  173.4 4.3 %fusion.75 = bf16[128,256,32]{1,2,0:T(8,128)(2,1)} fusion(bf16[32,64,128]{1,0,2:T(8,128)(2,1)S(1)} %copy-done.4, bf16[64,256,128]{1,0,2:T(8,128)(2,1)} %copy.51), kind=kOutput, calls=%fused_computation.136 | convolution fusion | flops 134217728 | bytes 6815744 | tf_op jit(solution)/shard_map/ijh,jkh->ikh/dot_general | solution.py:111
  177.7 4.6 %copy.56 = bf16[128,256,32]{0,1,2:T(8,128)(2,1)} copy(bf16[128,256,32]{1,2,0:T(8,128)(2,1)} %fusion.75) | data formatting | bytes 4194304 | tf_op jit(solution)/shard_map/ijh,jkh->ikh/dot_general | solution.py:111
  182.5 41.1 %reduce-scatter.7.cloned.1.call-done = bf16[8,32768]{1,0:T(8,128)(2,1)} async-done(((bf16[64,32768]{1,0:T(8,128)(2,1)}), bf16[8,32768]{1,0:T(8,128)(2,1)}) %reduce-scatter.7.cloned.1.call-update) | async-done | bytes 524304
  223.6 1.2 copy.71
  225.1 1.3 copy.58
  226.4 4.6 %all-to-all-start = ((bf16[1,8,256,128]{3,1,0,2:T(8,128)(2,1)}), bf16[1,8,256,128]{3,1,0,2:T(8,128)(2,1)}, u32[]{:S(2)}, u32[]{:S(2)}) async-start(bf16[1,8,256,128]{3,1,0,2:T(8,128)(2,1)} %copy.58), calls=%async_computation.1 | async-start | bytes 1048576 | tf_op jit(solution)/shard_map/all_to_all | solution.py:122
  231.1 1.8 fusion.51
  232.9 1.7 fusion.56
  234.6 1.1 copy.53
  235.7 23.9 %all-to-all-done = bf16[1,8,256,128]{3,1,0,2:T(8,128)(2,1)} async-done(((bf16[1,8,256,128]{3,1,0,2:T(8,128)(2,1)}), bf16[1,8,256,128]{3,1,0,2:T(8,128)(2,1)}, u32[]{:S(2)}, u32[]{:S(2)}) %all-to-all-start) | async-done | bytes 524320 | tf_op jit(solution)/shard_map/all_to_all | solution.py:122
  259.6 1.2 copy.60
  260.8 1.1 bitcast_multiply_fusion
  261.9 4.2 %all-to-all-start.1 = ((bf16[8,8,64,128]{3,2,1,0:T(8,128)(2,1)}), bf16[8,8,64,128]{3,2,1,0:T(8,128)(2,1)}, u32[]{:S(2)}, u32[]{:S(2)}) async-start(bf16[8,8,64,128]{3,2,1,0:T(8,128)(2,1)} %bitcast_multiply_fusion), calls=%async_computation.2 | async-start | bytes 2097152 | tf_op jit(solution)/shard_map/all_to_all | solution.py:127
  266.2 1.2 fusion.34
  269.7 11.9 %all-to-all-done.1 = bf16[8,8,64,128]{3,2,1,0:T(8,128)(2,1)} async-done(((bf16[8,8,64,128]{3,2,1,0:T(8,128)(2,1)}), bf16[8,8,64,128]{3,2,1,0:T(8,128)(2,1)}, u32[]{:S(2)}, u32[]{:S(2)}) %all-to-all-start.1) | async-done | bytes 1048608 | tf_op jit(solution)/shard_map/all_to_all | solution.py:127
  281.5 1.1 constant_dynamic-slice_fusion
  282.7 2.8 fusion.49
  286.5 1.4 convolution_add_fusion.1
  289.0 2.6 fusion.30
  291.6 11.8 %psum.94 = f32[4,128]{1,0:T(4,128)S(1)} all-reduce(f32[4,128]{1,0:T(4,128)S(1)} %pad_maximum_fusion.6), channel_id=1, replica_groups=mesh['row'=8,'col'=4] {'row'}, use_global_device_ids=true, to_apply=%region_24.25 | all-reduce | flops 512 | bytes 4096 | tf_op jit(solution)/shard_map/psum | solution.py:157
  303.4 10.3 %psum.95 = f32[4,128]{1,0:T(4,128)S(1)} all-reduce(f32[4,128]{1,0:T(4,128)S(1)} %psum.94), channel_id=1, replica_groups=mesh['row'=8,'col'=4] {'col'}, use_global_device_ids=true, to_apply=%region_25.26 | all-reduce | flops 512 | bytes 4096 | tf_op jit(solution)/shard_map/psum | solution.py:156
  313.7 52.4 %all-reduce.7.cloned.1.call-done = (f32[128,256]{1,0:T(8,128)}, f32[128,256]{1,0:T(8,128)}, f32[128,128]{1,0:T(8,128)}, f32[128,128]{1,0:T(8,128)}) async-done(((f32[128,256]{1,0:T(8,128)}, f32[128,256]{1,0:T(8,128)}, f32[128,128]{1,0:T(8,128)}, f32[128,128]{1,0:T(8,128)}), (f32[128,256]{1,0:T(8,128)}, f32[128,256]{1,0:T(8,128)}, f32[128,128]{1,0:T(8,128)}, ...) | async-done | bytes 393232 | tf_op jit(solution)/shard_map/psum | solution.py:157
  366.7 1.9 fusion.29
  368.6 36.3 %all-reduce.9.cloned.1.call-done = (f32[128,256]{1,0:T(8,128)}, f32[128,256]{1,0:T(8,128)}, f32[128,128]{1,0:T(8,128)}, f32[128,128]{1,0:T(8,128)}) async-done(((f32[128,256]{1,0:T(8,128)}, f32[128,256]{1,0:T(8,128)}, f32[128,128]{1,0:T(8,128)}, f32[128,128]{1,0:T(8,128)}), (f32[128,256]{1,0:T(8,128)}, f32[128,256]{1,0:T(8,128)}, f32[128,128]{1,0:T(8,128)}, ...) | async-done | bytes 393232 | tf_op jit(solution)/shard_map/psum | solution.py:156
  404.9 1.6 broadcast_multiply_fusion
  406.5 1.6 broadcast_multiply_fusion.1
  408.1 1.5 broadcast_multiply_fusion.2
  409.5 1.5 broadcast_multiply_fusion.3
  (70 shorter events, 8.7 us)
Async XLA Ops:
  7.2 137.9 %copy-start = (bf16[128,256]{1,0:T(8,128)(2,1)S(1)}, bf16[128,256]{1,0:T(8,128)(2,1)}, u32[]{:S(2)}) copy-start(bf16[128,256]{1,0:T(8,128)(2,1)} %param.17) | copy-start | bytes 196612
  7.2 5.7 %copy-start.12 = (bf16[128,128]{1,0:T(8,128)(2,1)S(1)}, bf16[128,128]{1,0:T(8,128)(2,1)}, u32[]{:S(2)}) copy-start(bf16[128,128]{1,0:T(8,128)(2,1)} %param.18) | copy-start | bytes 98308
  7.2 54.2 %all-gather.2.cloned.1.call-start = ((), (), s32[]{:S(2)}) async-start(), calls=%async_computation.4 | async-start | bytes 2621440 | tf_op jit(solution)/shard_map/all_gather | solution.py:75
  12.8 132.2 %all-reduce.11.cloned.1.call-start = ((), (), s32[]{:S(2)}) async-start(), calls=%async_computation.9 | async-start | bytes 8388608 | tf_op jit(solution)/shard_map/psum | solution.py:11
  65.2 1.0 copy-start.6
  65.2 1.0 copy-start.11
  65.2 158.4 %reduce-scatter.7.cloned.1.call-start = ((), (), s32[]{:S(2)}) async-start(), calls=%async_computation.6 | async-start | bytes 4718592
  67.6 4.0 copy-start.9
  164.8 0.7 copy-start.14
  165.5 1.3 copy-start.15
  166.8 1.8 copy-start.1
  168.6 1.3 copy-start.3
  172.2 1.2 copy-start.4
  172.2 110.4 %reduce-scatter.5.cloned.1.call-start = ((), (), s32[]{:S(2)}) async-start(), calls=%async_computation.5 | async-start | bytes 2621440 | tf_op jit(solution)/shard_map/reduce_scatter | solution.py:115
  223.6 7.5 %copy-start.2 = (bf16[32,64,128]{2,1,0:T(8,128)(2,1)S(1)}, bf16[32,64,128]{2,1,0:T(8,128)(2,1)}, u32[]{:S(2)}) copy-start(bf16[32,64,128]{2,1,0:T(8,128)(2,1)} %fusion.25) | copy-start | bytes 1572868
  226.4 33.2 %all-to-all-start = ((bf16[1,8,256,128]{3,1,0,2:T(8,128)(2,1)}), bf16[1,8,256,128]{3,1,0,2:T(8,128)(2,1)}, u32[]{:S(2)}, u32[]{:S(2)}) async-start(bf16[1,8,256,128]{3,1,0,2:T(8,128)(2,1)} %copy.58), calls=%async_computation.1 | async-start | bytes 1048576 | tf_op jit(solution)/shard_map/all_to_all | solution.py:122
  231.1 3.5 copy-start.8
  260.8 5.4 %copy-start.7 = (bf16[32,64,128]{2,1,0:T(8,128)(2,1)S(1)}, bf16[32,64,128]{2,1,0:T(8,128)(2,1)}, u32[]{:S(2)}) copy-start(bf16[32,64,128]{2,1,0:T(8,128)(2,1)} %param.12) | copy-start | bytes 1572868
  261.9 19.6 %all-to-all-start.1 = ((bf16[8,8,64,128]{3,2,1,0:T(8,128)(2,1)}), bf16[8,8,64,128]{3,2,1,0:T(8,128)(2,1)}, u32[]{:S(2)}, u32[]{:S(2)}) async-start(bf16[8,8,64,128]{3,2,1,0:T(8,128)(2,1)} %bitcast_multiply_fusion), calls=%async_computation.2 | async-start | bytes 2097152 | tf_op jit(solution)/shard_map/all_to_all | solution.py:127
  266.2 99.9 %all-reduce.7.cloned.1.call-start = ((), (), s32[]{:S(2)}) async-start(), calls=%async_computation.7 | async-start | bytes 786432 | tf_op jit(solution)/shard_map/psum | solution.py:157
  285.5 2.5 copy-start.10
  286.5 2.5 copy-start.5
  286.5 2.5 copy-start.13
  313.6 91.3 %all-reduce.9.cloned.1.call-start = ((), (), s32[]{:S(2)}) async-start(), calls=%async_computation.8 | async-start | bytes 786432 | tf_op jit(solution)/shard_map/psum | solution.py:156
Sparse Core Ops, SparseCore 0:
  13.0 48.3 all-gather.1
  65.4 79.6 all-reduce.10
  172.3 51.2 reduce-scatter.6
  225.7 51.5 reduce-scatter.4
  313.8 52.2 all-reduce.6
  368.6 36.3 all-reduce.8
